TPU v7x, 512 devices: a whole 4x4x16 slice. The times are simulated.
512 devices in a mesh: req: 32 (over z, core), mlp: 16 (over y, x).
Axes of the slice: x: 4, y: 4, z: 16, core: 2. Of those that a mesh axis runs over, the one named last changes fastest.
Arguments:
- hidden_input: bfloat16 [12288, 4096], P('req', 'mlp'), may hold values from -6 to 6
- input_norm_gain: bfloat16 [4096], replicated, may hold values from 0.099609375 to 1.8984375
- query_norm_gain: bfloat16 [128], replicated, may hold values from 0.099609375 to 1.8984375
- key_norm_gain: bfloat16 [128], replicated, may hold values from 0.099609375 to 1.8984375
- query_weight: bfloat16 [4096, 4096], P('req', 'mlp'), may hold values from -0.09375 to 0.09375
- key_value_weight: bfloat16 [4096, 2, 1024], P('req'), may hold values from -0.09375 to 0.09375
- output_weight: bfloat16 [4096, 16, 256], P('mlp', None, 'req'), may hold values from -0.09375 to 0.09375
- adapter_down_qkv: bfloat16 [64, 48, 4096], P('req', None, 'mlp'), may hold values from -0.09375 to 0.09375
- adapter_down_output: bfloat16 [64, 16, 4096], P('req', None, 'mlp'), may hold values from -0.09375 to 0.09375
- adapter_up_query: bfloat16 [64, 16, 4096], P('req', None, 'mlp'), may hold values from -1.5 to 1.5
- adapter_up_key_value: bfloat16 [64, 16, 2, 1024], P('req'), may hold values from -1.5 to 1.5
- adapter_up_output: bfloat16 [64, 16, 4096], P('req', None, 'mlp'), may hold values from -1.5 to 1.5
- pool: bfloat16 [16384, 2, 1024], P('req'), may hold values from -6 to 6
- lengths: int32 [32, 4], P('req'), may hold values from 1 to 192, 384 in all within a row
- cached_prefix_pages: int32 [32, 4], P('req'), may hold values from 0 to 8
- prefix_page_table: int32 [32, 4, 8], P('req'), may hold values from 0 to 7, each once within a row
- adapter_of_request: int32 [32, 4, 1], P('req'), may hold values from 0 to 63
- adapter_storage: int32 [64], replicated, may hold values from 0 to 63, each once
Outputs:
- attention_update: bfloat16 [12288, 4096], P('req', 'mlp')
- new_cache: bfloat16 [12288, 2, 1024], P('req', None, 'mlp')
Inputs may be any that keep to these rules, and one draw needn't show every extreme that they name: The lengths of one index of req sum to 384, and the longest of them is 192. `prefix_page_table`: each row lists every page of its pool once. `adapter_of_request`: every adapter is used by some request. `adapter_storage`: each slot holds one adapter.
All inputs are finite; a program needn't handle non-finite values.
Results may differ from a plain program's by a relative error of at most 0.035.
Values may be sent and summed in bfloat16 or wider, within the bound.
A program may use at most 64 MiB of HBM per device.

v0:
```python
import math
import jax
import jax.numpy as jnp
from jax import lax
from jax.sharding import PartitionSpec as P

QUERY_HEADS = 32
KEY_VALUE_HEADS = 8
HEAD_SIZE = 128
ADAPTER_RANK = 16
PAGE = 64
epsilon = 1e-06
rope_base = 1000000.0


def root_mean_scale(values, gain_vec):
    mean_sq = jnp.mean(values * values, axis=-1, keepdims=True)
    return values * lax.rsqrt(mean_sq + epsilon) * gain_vec.astype(jnp.float32)


def rotary_embed(values, token_positions):
    half_width = values.shape[-1] // 2
    inverse_freq = jnp.exp(
        jnp.arange(half_width, dtype=jnp.float32) * (-2.0 / values.shape[-1]) * math.log(rope_base)
    )
    angles = token_positions.astype(jnp.float32)[:, None] * inverse_freq[None, :]
    cosine = jnp.cos(angles)[:, None, :]
    sine_part = jnp.sin(angles)[:, None, :]
    front = values[..., :half_width]
    back = values[..., half_width:]
    return jnp.concatenate(
        [front * cosine - back * sine_part, back * cosine + front * sine_part], axis=-1
    )


def row_tables(lengths_row, prefix_row, page_rows, row_count):
    ends_at = jnp.cumsum(lengths_row)
    starts_at = ends_at - lengths_row
    row_ids = jnp.arange(row_count, dtype=jnp.int32)
    owners = jnp.sum((row_ids[:, None] >= ends_at[None, :]).astype(jnp.int32), axis=1)
    group_members = owners[:, None] == jnp.arange(lengths_row.shape[0], dtype=jnp.int32)[None, :]
    offsets = PAGE * prefix_row[None, :] + row_ids[:, None] - starts_at[None, :]
    token_positions = jnp.sum(jnp.where(group_members, offsets, 0), axis=1)
    page_ids = jnp.arange(page_rows.shape[1], dtype=jnp.int32)
    listed = (page_rows[:, :, None] == page_ids[None, None, :]) & (
        page_ids[None, :, None] < prefix_row[:, None, None]
    )
    page_used = jnp.sum(listed.astype(jnp.float32), axis=1)
    return (owners, group_members, token_positions, page_used)


def apply_adapter(lowrank_inner, group_members, chosen_up):
    masked = lowrank_inner[:, None, :] * group_members.astype(lowrank_inner.dtype)[:, :, None]
    return jnp.einsum("gjr,jrc->gc", masked, chosen_up, preferred_element_type=jnp.float32)


def select_rows(terms, group_members):
    return jnp.sum(terms * group_members.astype(jnp.float32)[:, :, None], axis=1)


def shards(
    hidden_input,
    input_norm_gain,
    query_norm_gain,
    key_norm_gain,
    query_weight,
    key_value_weight,
    output_weight,
    adapter_down_qkv,
    adapter_down_output,
    adapter_up_query,
    adapter_up_key_value,
    adapter_up_output,
    pool,
    lengths,
    cached_prefix_pages,
    prefix_page_table,
    adapter_of_request,
    adapter_storage,
):
    feature_group_count = lax.axis_size("mlp")
    feature_group_index = lax.axis_index("mlp")
    whole = lax.all_gather(hidden_input, "mlp", axis=1, tiled=True)
    row_count, full_width = whole.shape
    normalized_input = root_mean_scale(whole.astype(jnp.float32), input_norm_gain).astype(
        jnp.bfloat16
    )
    owners, group_members, token_positions, page_used = row_tables(
        lengths[0], cached_prefix_pages[0], prefix_page_table[0], row_count
    )
    q_width = query_weight.shape[1]
    query_head_rows = q_width // HEAD_SIZE
    key_value_local = max(1, KEY_VALUE_HEADS // feature_group_count)
    key_value_width = key_value_local * HEAD_SIZE
    key_value_begin = (
        feature_group_index * query_head_rows // (QUERY_HEADS // KEY_VALUE_HEADS) * HEAD_SIZE
    )
    own_wkv = lax.dynamic_slice_in_dim(key_value_weight, key_value_begin, key_value_width, 2)
    request_key_value_up = lax.dynamic_slice_in_dim(
        adapter_up_key_value, key_value_begin, key_value_width, 3
    )
    gathered = (
        lax.all_gather(adapter_down_qkv, "req", axis=0, tiled=True),
        lax.all_gather(adapter_down_output, "req", axis=0, tiled=True),
        lax.all_gather(adapter_up_query, "req", axis=0, tiled=True),
        lax.all_gather(request_key_value_up, "req", axis=0, tiled=True),
        lax.all_gather(adapter_up_output, "req", axis=0, tiled=True),
    )
    slot_indices = jnp.take(adapter_storage, adapter_of_request[0, :, 0], axis=0)
    chosen_down = jnp.take(gathered[0], slot_indices, axis=0)
    output_down = jnp.take(gathered[1], slot_indices, axis=0)
    query_up_part = jnp.take(gathered[2], slot_indices, axis=0)
    key_value_up = jnp.take(gathered[3], slot_indices, axis=0)
    output_up = jnp.take(gathered[4], slot_indices, axis=0)
    feature_cols = full_width // feature_group_count
    own_normed = lax.dynamic_slice_in_dim(
        normalized_input, feature_group_index * feature_cols, feature_cols, 1
    )
    low_terms = jnp.einsum(
        "gd,jkd->gjk", own_normed, chosen_down, preferred_element_type=jnp.float32
    )
    lowrank_inner = lax.psum(select_rows(low_terms, group_members).astype(jnp.bfloat16), "mlp")
    q_part = lax.all_gather(query_weight, "req", axis=0, tiled=True)
    kv_part = lax.all_gather(own_wkv, "req", axis=0, tiled=True)
    query_width_total = jnp.dot(normalized_input, q_part, preferred_element_type=jnp.float32)
    kv_total = jnp.dot(
        normalized_input,
        kv_part.reshape(kv_part.shape[0], 2 * key_value_width),
        preferred_element_type=jnp.float32,
    )
    query_width_total, kv_total = (query_width_total, kv_total)
    query_plain = (
        query_width_total
        + apply_adapter(lowrank_inner[:, 0:ADAPTER_RANK], group_members, query_up_part)
    ).astype(jnp.bfloat16)
    key_lowrank_part = apply_adapter(
        lowrank_inner[:, ADAPTER_RANK : 2 * ADAPTER_RANK], group_members, key_value_up[:, :, 0]
    )
    value_lowrank_part = apply_adapter(
        lowrank_inner[:, 2 * ADAPTER_RANK : 3 * ADAPTER_RANK], group_members, key_value_up[:, :, 1]
    )
    key_value_plain = (
        kv_total.reshape(row_count, 2, key_value_width)
        + jnp.stack([key_lowrank_part, value_lowrank_part], axis=1)
    ).astype(jnp.bfloat16)
    cached = lax.dynamic_slice_in_dim(pool, key_value_begin, key_value_width, 2)
    pool_token_rows = cached.shape[0]
    query_rotated = rotary_embed(
        root_mean_scale(
            query_plain.astype(jnp.float32).reshape(row_count, query_head_rows, HEAD_SIZE),
            query_norm_gain,
        ),
        token_positions,
    ).astype(jnp.bfloat16)
    key_rotated = rotary_embed(
        root_mean_scale(
            key_value_plain[:, 0]
            .astype(jnp.float32)
            .reshape(row_count, key_value_local, HEAD_SIZE),
            key_norm_gain,
        ),
        token_positions,
    ).astype(jnp.bfloat16)
    cache_columns = KEY_VALUE_HEADS * HEAD_SIZE // feature_group_count
    own_offset = feature_group_index * cache_columns - key_value_begin
    local_cache = jnp.stack(
        [key_rotated.reshape(row_count, key_value_width), key_value_plain[:, 1]], axis=1
    )
    new_cache = lax.dynamic_slice_in_dim(local_cache, own_offset, cache_columns, 2)
    key_matrix = jnp.concatenate(
        [cached[:, 0].reshape(pool_token_rows, key_value_local, HEAD_SIZE), key_rotated], axis=0
    )
    value_matrix = jnp.concatenate(
        [
            cached[:, 1].reshape(pool_token_rows, key_value_local, HEAD_SIZE),
            key_value_plain[:, 1].reshape(row_count, key_value_local, HEAD_SIZE),
        ],
        axis=0,
    )
    pool_ok = jnp.dot(group_members.astype(jnp.float32), page_used, precision=lax.Precision.HIGHEST)
    pool_ok = jnp.repeat(pool_ok, PAGE, axis=1) > 0.5
    row_ids = jnp.arange(row_count, dtype=jnp.int32)
    causal = (owners[:, None] == owners[None, :]) & (row_ids[None, :] <= row_ids[:, None])
    allowed = jnp.concatenate([pool_ok, causal], axis=1)
    query_rows = query_rotated.reshape(
        row_count, key_value_local, query_head_rows // key_value_local, HEAD_SIZE
    )
    scores = jnp.einsum(
        "gkhd,skd->khgs", query_rows, key_matrix, preferred_element_type=jnp.float32
    ) / math.sqrt(HEAD_SIZE)
    exp_scores = jnp.where(allowed[None, None], jnp.exp(scores), 0.0)
    softmax = (exp_scores / jnp.sum(exp_scores, axis=-1, keepdims=True)).astype(jnp.bfloat16)
    attended = jnp.einsum(
        "khgs,skd->gkhd", softmax, value_matrix, preferred_element_type=jnp.float32
    )
    attended = attended.astype(jnp.bfloat16).reshape(row_count, q_width)
    out_terms = jnp.einsum("gc,jrc->gjr", attended, output_down, preferred_element_type=jnp.float32)
    lowrank_result = lax.psum(select_rows(out_terms, group_members), "mlp").astype(jnp.bfloat16)
    partial_value = jnp.einsum(
        "gc,cnk->gnk",
        attended,
        lax.all_gather(output_weight, "req", axis=2, tiled=True),
        preferred_element_type=jnp.float32,
    )
    summed_output = lax.psum_scatter(
        partial_value.reshape(row_count, full_width).astype(jnp.bfloat16),
        "mlp",
        scatter_dimension=1,
        tiled=True,
    ).astype(jnp.float32)
    attention_update = (
        summed_output + apply_adapter(lowrank_result, group_members, output_up)
    ).astype(jnp.bfloat16)
    return (attention_update, new_cache)


def solution(mesh):
    return jax.shard_map(
        shards,
        mesh=mesh,
        in_specs=(
            P("req", "mlp"),
            P(),
            P(),
            P(),
            P("req", "mlp"),
            P("req", None, None),
            P("mlp", None, "req"),
            P("req", None, "mlp"),
            P("req", None, "mlp"),
            P("req", None, "mlp"),
            P("req", None, None, None),
            P("req", None, "mlp"),
            P("req", None, None),
            P("req", None),
            P("req", None),
            P("req", None, None),
            P("req", None, None),
            P(),
        ),
        out_specs=(P("req", "mlp"), P("req", None, "mlp")),
        check_vma=False,
    )
```

profile of v0, /device:TPU:32, one launch (start us, length us, event | category | flops | bytes accessed | tf_op | source)
XLA Modules:
  0.0 518.9 jit_solution(2938642543624137017)
XLA Ops:
  7.3 0.7 all-gather.10.cloned.1.call-update
  8.0 0.2 copy-done
  8.2 0.7 constant_dynamic-slice_fusion.2
  9.0 0.7 all-gather.6.cloned.1.call-update
  9.7 0.5 all-gather.12.cloned.1.call-update
  10.3 0.5 all-gather.14.cloned.1.call-update
  10.9 0.7 fusion.90
  11.6 1.3 gather_fusion
  12.9 0.7 fusion.80
  13.5 0.7 compare_and_fusion
  14.2 0.8 reduce-window.4
  15.0 0.7 fusion.81
  15.8 0.6 fusion.76
  16.4 0.1 fusion.28
  16.5 0.7 constant_dynamic-slice_fusion.1
  17.3 36.1 %all_gather.30 = bf16[64,16,2,128]{3,1,2,0:T(8,128)(2,1)S(1)} all-gather(bf16[2,16,2,128]{3,1,2,0:T(8,128)(2,1)S(1)} %copy.66), channel_id=1, replica_groups=mesh['req'=32,'mlp'=16] {'req'}, dimensions={0}, use_global_device_ids=true | all-gather | bytes 540672 | tf_op jit(solution)/shard_map/all_gather | solution.py:106
  53.3 0.7 convert_element_type.100
  54.0 1.2 convert_element_type.109
  55.2 0.7 multiply_bitcast_fusion
  55.9 0.1 select_reduce_fusion
  56.0 1.6 constant_dynamic-slice_fusion
  57.6 30.2 %all_gather.32 = bf16[64,16,256]{2,1,0:T(8,128)(2,1)S(1)} all-gather(bf16[2,16,256]{2,1,0:T(8,128)(2,1)S(1)} %copy-done.6), channel_id=1, replica_groups=mesh['req'=32,'mlp'=16] {'req'}, dimensions={0}, use_global_device_ids=true | all-gather | bytes 540672 | tf_op jit(solution)/shard_map/all_gather | solution.py:105
  87.8 0.5 convert_element_type.112
  88.4 0.1 convert_reduce_fusion
  88.5 0.2 convolution_compare_fusion
  88.7 0.7 copy.65
  89.4 0.6 gather_fusion.2
  90.0 0.7 copy_select_fusion
  90.7 1.2 gather_fusion.3
  91.8 0.8 multiply_cosine_fusion
  92.8 2.6 gather_fusion.1
  95.4 61.2 %all-gather.8.cloned.1.call-done = bf16[4096,2,128]{2,1,0:T(2,128)(2,1)} async-done(((bf16[128,2,128]{2,1,0:T(2,128)(2,1)}), bf16[4096,2,128]{2,1,0:T(2,128)(2,1)}) %all-gather.8.cloned.1.call-update) | async-done | bytes 2097168 | tf_op jit(solution)/shard_map/all_gather | solution.py:124
  156.6 4.7 copy.61
  161.3 63.1 %all-gather.6.cloned.1.call-done = bf16[384,4096]{1,0:T(8,128)(2,1)} async-done(((bf16[384,256]{1,0:T(8,128)(2,1)}), bf16[384,4096]{1,0:T(8,128)(2,1)}) %all-gather.6.cloned.1.call-update) | async-done | bytes 3145744 | tf_op jit(solution)/shard_map/all_gather | solution.py:83
  224.4 2.7 fusion
  227.2 0.1 copy-done.1
  227.3 1.1 fusion.2
  228.4 1.6 copy-done.2
  230.0 0.9 fusion.26
  230.9 72.8 %psum.14 = bf16[384,48]{0,1:T(8,128)(2,1)S(1)} all-reduce(bf16[384,48]{0,1:T(8,128)(2,1)} %fusion.26), channel_id=1, replica_groups=mesh['req'=32,'mlp'=16] {'mlp'}, use_global_device_ids=true, to_apply=%region_4.5 | all-reduce | flops 18432 | bytes 73728 | tf_op jit(solution)/shard_map/psum | solution.py:122
  303.7 0.9 convolution_bitcast_fusion.2
  304.7 0.9 convolution_bitcast_fusion.3
  305.6 3.2 fusion.17
  309.0 0.4 fusion.46
  309.5 0.1 copy.53
  309.6 3.8 fusion.92
  313.5 0.4 multiply_reduce_fusion
  313.8 0.1 copy.54
  314.0 0.1 copy.52
  314.1 0.2 multiply_multiply_fusion
  314.3 0.2 subtract_convert_fusion
  314.5 0.9 fusion.5
  315.5 0.9 fusion.23
  316.4 53.5 %all-gather.14.cloned.1.call-done = bf16[256,16,256]{0,2,1:T(8,128)(2,1)} async-done(((bf16[256,16,8]{0,2,1:T(8,128)(2,1)}), bf16[256,16,256]{0,2,1:T(8,128)(2,1)}) %all-gather.14.cloned.1.call-update) | async-done | bytes 2097168 | tf_op jit(solution)/shard_map/all_gather | solution.py:202
  369.9 4.3 convolution_convert_fusion
  374.2 0.7 copy-done.7
  374.9 28.9 %all_gather.34 = bf16[64,16,256]{2,1,0:T(8,128)(2,1)S(1)} all-gather(bf16[2,16,256]{2,1,0:T(8,128)(2,1)S(1)} %copy-done.7), channel_id=1, replica_groups=mesh['req'=32,'mlp'=16] {'req'}, dimensions={0}, use_global_device_ids=true | all-gather | bytes 540672 | tf_op jit(solution)/shard_map/all_gather | solution.py:104
  403.8 0.5 gather_fusion.4
  404.3 30.1 %all_gather.35 = bf16[64,16,256]{2,1,0:T(8,128)(2,1)S(1)} all-gather(bf16[2,16,256]{2,1,0:T(8,128)(2,1)S(1)} %copy-done.8), channel_id=1, replica_groups=mesh['req'=32,'mlp'=16] {'req'}, dimensions={0}, use_global_device_ids=true | all-gather | bytes 540672 | tf_op jit(solution)/shard_map/all_gather | solution.py:107
  434.4 0.5 gather_fusion.5
  435.0 0.2 fusion.27
  435.2 74.3 %psum.15 = bf16[384,16]{0,1:T(8,128)(2,1)S(1)} all-reduce(f32[384,16]{0,1:T(8,128)S(1)} %fusion.27), channel_id=1, replica_groups=mesh['req'=32,'mlp'=16] {'mlp'}, use_global_device_ids=true, to_apply=%region_12.14 | all-reduce | flops 6144 | bytes 36864 | tf_op jit(solution)/shard_map/psum | solution.py:198
  509.5 0.7 fusion.50
  510.2 1.9 fusion.16
  (62 shorter events, 0.9 us)
Async XLA Ops:
  7.2 1.1 copy-start
  7.2 81.2 %copy-start.17 = (s32[1,4]{1,0:T(1,128)S(1)}, s32[1,4]{1,0:T(1,128)}, u32[]{:S(2)}) copy-start(s32[1,4]{1,0:T(1,128)} %param.34) | copy-start | bytes 52
  7.2 50.4 %copy-start.6 = (bf16[2,16,256]{2,1,0:T(8,128)(2,1)S(1)}, bf16[2,16,256]{2,1,0:T(8,128)(2,1)}, u32[]{:S(2)}) copy-start(bf16[2,16,256]{2,1,0:T(8,128)(2,1)} %param.29) | copy-start | bytes 49156
  7.2 80.6 %copy-start.16 = (bf16[128]{0:T(256)(128)(2,1)S(1)}, bf16[128]{0:T(256)(128)(2,1)}, u32[]{:S(2)}) copy-start(bf16[128]{0:T(256)(128)(2,1)} %param.22) | copy-start | bytes 772
  7.2 81.2 %copy-start.13 = (s32[1,4,8]{2,1,0:T(4,128)S(1)}, s32[1,4,8]{2,1,0:T(4,128)}, u32[]{:S(2)}) copy-start(s32[1,4,8]{2,1,0:T(4,128)} %param.35) | copy-start | bytes 388
  7.2 85.5 %all-gather.10.cloned.1.call-start = ((), (), s32[]{:S(2)}) async-start(), calls=%async_computation.3 | async-start | bytes 1622016 | tf_op jit(solution)/shard_map/all_gather | solution.py:103
  8.0 148.6 %all-gather.8.cloned.1.call-start = ((), (), s32[]{:S(2)}) async-start(), calls=%async_computation.2 | async-start | bytes 2162688 | tf_op jit(solution)/shard_map/all_gather | solution.py:124
  8.9 215.5 %all-gather.6.cloned.1.call-start = ((), (), s32[]{:S(2)}) async-start(), calls=%async_computation.1 | async-start | bytes 3342336 | tf_op jit(solution)/shard_map/all_gather | solution.py:83
  9.7 299.9 %all-gather.12.cloned.1.call-start = ((), (), s32[]{:S(2)}) async-start(), calls=%async_computation.4 | async-start | bytes 2162688 | tf_op jit(solution)/shard_map/all_gather | solution.py:123
  10.3 359.6 %all-gather.14.cloned.1.call-start = ((), (), s32[]{:S(2)}) async-start(), calls=%async_computation.5 | async-start | bytes 2162688 | tf_op jit(solution)/shard_map/all_gather | solution.py:202
  10.8 499.4 %reduce-scatter.2.cloned.1.call-start = ((), (), s32[]{:S(2)}) async-start(), calls=%async_computation.6 | async-start | bytes 3342336 | tf_op jit(solution)/shard_map/reduce_scatter | solution.py:205
  14.2 147.1 %copy-start.11 = (f32[64]{0:T(128)}, f32[64]{0:T(128)S(1)}, u32[]{:S(2)}) copy-start(f32[64]{0:T(128)S(1)} %multiply_exponential_fusion) | copy-start | bytes 772
  224.4 2.8 copy-start.1
  227.3 2.8 copy-start.5
  227.3 2.8 copy-start.9
  228.4 1.7 copy-start.2
  305.6 3.3 copy-start.14
  305.6 3.4 copy-start.12
  309.6 3.9 copy-start.4
  309.6 4.5 copy-start.15
  314.3 1.2 copy-start.3
  374.1 0.7 copy-start.7
  374.1 30.2 %copy-start.8 = (bf16[2,16,256]{2,1,0:T(8,128)(2,1)S(1)}, bf16[2,16,256]{2,1,0:T(8,128)(2,1)}, u32[]{:S(2)}) copy-start(bf16[2,16,256]{2,1,0:T(8,128)(2,1)} %param.31) | copy-start | bytes 49156
  374.1 60.9 %copy-start.10 = (f32[384,4]{0,1:T(4,128)S(1)}, f32[384,4]{0,1:T(4,128)}, u32[]{:S(2)}) copy-start(f32[384,4]{0,1:T(4,128)} %get-tuple-element.17) | copy-start | bytes 18436
Sparse Core Ops, SparseCore 0:
  10.2 75.3 all-gather.9
  87.7 68.8 all-gather.7
  159.6 64.8 all-gather.5
  226.4 71.1 all-gather.11
  299.5 70.3 all-gather.13
  374.3 87.2 reduce-scatter.1
where the time goes:
time: 520 us; the launch traced here: 519 us
  blocking collectives  272 us (52%)
  waiting for transfers between devices  180 us (35%)
  matrix products  18.5 us (4%)
  local copies, waits for them, and re-layouts  18.3 us (4%)
  other arithmetic  14.7 us (3%)
  between operations  14.6 us (3%)
    psum x1, blocking collectives, shards(): lax.psum(select_rows(out_terms, group_members), 'mlp').astype(jnp.bfloat16)  74.3 us
    psum x1, blocking collectives, shards(): lax.psum(select_rows(low_terms, group_members).astype(jnp.bfloat16), 'mlp')  72.8 us
    all_gather x1, waiting for transfers between devices, shards(): whole = lax.all_gather(hidden_input, 'mlp', axis=1, tiled=True)  63.1 us
    all_gather x1, waiting for transfers between devices, shards(): kv_part = lax.all_gather(own_wkv, 'req', axis=0, tiled=True)  61.2 us
    all_gather x1, waiting for transfers between devices, shards(): lax.all_gather(output_weight, 'req', axis=2, tiled=True)  53.5 us
    all_gather x1, blocking collectives, shards(): lax.all_gather(request_key_value_up, 'req', axis=0, tiled=True)  36.1 us
    all_gather x1, blocking collectives, shards(): lax.all_gather(adapter_up_query, 'req', axis=0, tiled=True)  30.2 us
    all_gather x1, blocking collectives, shards(): lax.all_gather(adapter_up_output, 'req', axis=0, tiled=True)  30.1 us
  transfers between devices with their start and end apart: 6, of which 3 were waited for; matrix products, arithmetic and copies ran while one was open for 8% of the time, Pallas kernels for 0%

commit v1 on v0

--- a/solution.py
+++ b/solution.py
@@ -195,7 +195,9 @@
     )
     attended = attended.astype(jnp.bfloat16).reshape(row_count, q_width)
     out_terms = jnp.einsum("gc,jrc->gjr", attended, output_down, preferred_element_type=jnp.float32)
-    lowrank_result = lax.psum(select_rows(out_terms, group_members), "mlp").astype(jnp.bfloat16)
+    lowrank_result = jnp.sum(
+        lax.all_gather(select_rows(out_terms, group_members), "mlp"), axis=0
+    ).astype(jnp.bfloat16)
     partial_value = jnp.einsum(
         "gc,cnk->gnk",
         attended,

time: 520 us -> 471 us (0.906)
  blocking collectives: 272 us -> 223 us
    psum x1 -> x0, blocking collectives: 74.3 us -> none  [shards(): lax.psum(select_rows(out_terms, group_members), 'mlp').astype(jnp.bfloat16)]
    all_gather x0 -> x1, blocking collectives: none -> 24.6 us  [shards(): lax.all_gather(select_rows(out_terms, group_members), 'mlp')]
  transfers between devices with their start and end apart: 6 -> 6, of which waited for: 3 -> 4; matrix products, arithmetic and copies ran while one was open for 8% -> 9% of each run, Pallas kernels for 0% -> 0%
where the time goes in v1:
time: 471 us; the launch traced here: 470 us
  blocking collectives  223 us (47%)
  waiting for transfers between devices  181 us (38%)
  matrix products  18.5 us (4%)
  local copies, waits for them, and re-layouts  18.4 us (4%)
  other arithmetic  14.8 us (3%)
  between operations  14.6 us (3%)
    psum x1, blocking collectives, shards(): lax.psum(select_rows(low_terms, group_members).astype(jnp.bfloat16), 'mlp')  72.8 us
    all_gather x1, waiting for transfers between devices, shards(): whole = lax.all_gather(hidden_input, 'mlp', axis=1, tiled=True)  63.1 us
    all_gather x1, waiting for transfers between devices, shards(): kv_part = lax.all_gather(own_wkv, 'req', axis=0, tiled=True)  61.2 us
    all_gather x1, waiting for transfers between devices, shards(): lax.all_gather(output_weight, 'req', axis=2, tiled=True)  53.5 us
    all_gather x1, blocking collectives, shards(): lax.all_gather(request_key_value_up, 'req', axis=0, tiled=True)  36.1 us
    all_gather x1, blocking collectives, shards(): lax.all_gather(adapter_up_query, 'req', axis=0, tiled=True)  30.2 us
    all_gather x1, blocking collectives, shards(): lax.all_gather(adapter_up_output, 'req', axis=0, tiled=True)  30.1 us
    all_gather x1, blocking collectives, shards(): lax.all_gather(adapter_down_output, 'req', axis=0, tiled=True)  28.9 us
  transfers between devices with their start and end apart: 6, of which 4 were waited for; matrix products, arithmetic and copies ran while one was open for 9% of the time, Pallas kernels for 0%

profile of v1, /device:TPU:32, one launch (start us, length us, event | category | flops | bytes accessed | tf_op | source)
XLA Modules:
  0.0 470.5 jit_solution(2442774140966640459)
XLA Ops:
  7.3 0.7 all-gather.11.cloned.1.call-update
  8.0 0.2 copy-done
  8.2 0.7 constant_dynamic-slice_fusion.2
  9.0 0.7 all-gather.7.cloned.1.call-update
  9.7 0.5 all-gather.13.cloned.1.call-update
  10.3 0.5 all-gather.15.cloned.1.call-update
  10.9 0.7 fusion.90
  11.6 1.3 gather_fusion
  12.9 0.7 fusion.80
  13.5 0.7 compare_and_fusion
  14.2 0.8 reduce-window.4
  15.0 0.7 fusion.81
  15.8 0.6 fusion.76
  16.4 0.1 fusion.28
  16.5 0.7 constant_dynamic-slice_fusion.1
  17.3 36.1 %all_gather.36 = bf16[64,16,2,128]{3,1,2,0:T(8,128)(2,1)S(1)} all-gather(bf16[2,16,2,128]{3,1,2,0:T(8,128)(2,1)S(1)} %copy.66), channel_id=1, replica_groups=mesh['req'=32,'mlp'=16] {'req'}, dimensions={0}, use_global_device_ids=true | all-gather | bytes 540672 | tf_op jit(solution)/shard_map/all_gather | solution.py:106
  53.3 0.7 convert_element_type.104
  54.0 1.2 convert_element_type.113
  55.2 0.7 multiply_bitcast_fusion
  56.0 1.6 constant_dynamic-slice_fusion
  57.6 30.2 %all_gather.38 = bf16[64,16,256]{2,1,0:T(8,128)(2,1)S(1)} all-gather(bf16[2,16,256]{2,1,0:T(8,128)(2,1)S(1)} %copy-done.6), channel_id=1, replica_groups=mesh['req'=32,'mlp'=16] {'req'}, dimensions={0}, use_global_device_ids=true | all-gather | bytes 540672 | tf_op jit(solution)/shard_map/all_gather | solution.py:105
  87.8 0.5 convert_element_type.116
  88.4 0.1 convert_reduce_fusion
  88.5 0.2 convolution_compare_fusion
  88.7 0.7 copy.65
  89.4 0.6 gather_fusion.2
  90.0 0.7 copy_select_fusion
  90.7 1.2 gather_fusion.3
  91.8 0.8 multiply_cosine_fusion
  92.8 2.6 gather_fusion.1
  95.4 61.2 %all-gather.9.cloned.1.call-done = bf16[4096,2,128]{2,1,0:T(2,128)(2,1)} async-done(((bf16[128,2,128]{2,1,0:T(2,128)(2,1)}), bf16[4096,2,128]{2,1,0:T(2,128)(2,1)}) %all-gather.9.cloned.1.call-update) | async-done | bytes 2097168 | tf_op jit(solution)/shard_map/all_gather | solution.py:124
  156.6 4.7 %copy.61 = bf16[4096,2,128]{0,2,1:T(8,128)(2,1)S(1)} copy(bf16[4096,2,128]{2,1,0:T(2,128)(2,1)} %all-gather.9.cloned.1.call-done) | data formatting | bytes 4194304 | tf_op jit(solution)/shard_map/reshape | solution.py:128
  161.3 63.1 %all-gather.7.cloned.1.call-done = bf16[384,4096]{1,0:T(8,128)(2,1)} async-done(((bf16[384,256]{1,0:T(8,128)(2,1)}), bf16[384,4096]{1,0:T(8,128)(2,1)}) %all-gather.7.cloned.1.call-update) | async-done | bytes 3145744 | tf_op jit(solution)/shard_map/all_gather | solution.py:83
  224.4 2.7 fusion
  227.2 0.1 copy-done.1
  227.3 1.1 fusion.2
  228.4 1.6 copy-done.2
  230.0 0.9 fusion.26
  230.9 72.8 %psum.7 = bf16[384,48]{0,1:T(8,128)(2,1)S(1)} all-reduce(bf16[384,48]{0,1:T(8,128)(2,1)} %fusion.26), channel_id=1, replica_groups=mesh['req'=32,'mlp'=16] {'mlp'}, use_global_device_ids=true, to_apply=%region_4.5 | all-reduce | flops 18432 | bytes 73728 | tf_op jit(solution)/shard_map/psum | solution.py:122
  303.7 0.9 convolution_bitcast_fusion.2
  304.7 0.9 convolution_bitcast_fusion.3
  305.6 3.2 fusion.17
  309.0 0.4 fusion.46
  309.5 0.1 copy.53
  309.6 3.8 fusion.92
  313.5 0.4 multiply_reduce_fusion
  313.8 0.1 copy.54
  314.0 0.1 copy.52
  314.1 0.2 multiply_multiply_fusion
  314.3 0.2 subtract_convert_fusion
  314.5 0.9 fusion.5
  315.5 0.9 fusion.23
  316.4 53.5 %all-gather.15.cloned.1.call-done = bf16[256,16,256]{0,2,1:T(8,128)(2,1)} async-done(((bf16[256,16,8]{0,2,1:T(8,128)(2,1)}), bf16[256,16,256]{0,2,1:T(8,128)(2,1)}) %all-gather.15.cloned.1.call-update) | async-done | bytes 2097168 | tf_op jit(solution)/shard_map/all_gather | solution.py:204
  369.9 4.3 convolution_convert_fusion
  374.2 0.7 copy-done.7
  374.9 28.9 %all_gather.40 = bf16[64,16,256]{2,1,0:T(8,128)(2,1)S(1)} all-gather(bf16[2,16,256]{2,1,0:T(8,128)(2,1)S(1)} %copy-done.7), channel_id=1, replica_groups=mesh['req'=32,'mlp'=16] {'req'}, dimensions={0}, use_global_device_ids=true | all-gather | bytes 540672 | tf_op jit(solution)/shard_map/all_gather | solution.py:104
  403.8 0.5 gather_fusion.4
  404.3 30.1 %all_gather.43 = bf16[64,16,256]{2,1,0:T(8,128)(2,1)S(1)} all-gather(bf16[2,16,256]{2,1,0:T(8,128)(2,1)S(1)} %copy-done.8), channel_id=1, replica_groups=mesh['req'=32,'mlp'=16] {'req'}, dimensions={0}, use_global_device_ids=true | all-gather | bytes 540672 | tf_op jit(solution)/shard_map/all_gather | solution.py:107
  434.4 0.5 gather_fusion.5
  435.0 0.2 fusion.27
  435.2 24.6 %all-gather = f32[6144,16]{0,1:T(8,128)S(1)} all-gather(f32[384,16]{0,1:T(8,128)S(1)} %fusion.27), channel_id=2, replica_groups=mesh['req'=32,'mlp'=16] {'mlp'}, dimensions={0}, use_global_device_ids=true | all-gather | bytes 417792 | tf_op jit(solution)/shard_map/all_gather | solution.py:199
  459.9 0.7 fusion.50
  460.7 1.1 reduce-scatter.2.cloned.1.call-done
  461.8 1.9 fusion.16
  (64 shorter events, 1.2 us)
Async XLA Ops:
  7.2 1.1 copy-start
  7.2 81.2 %copy-start.17 = (s32[1,4]{1,0:T(1,128)S(1)}, s32[1,4]{1,0:T(1,128)}, u32[]{:S(2)}) copy-start(s32[1,4]{1,0:T(1,128)} %param.34) | copy-start | bytes 52
  7.2 50.4 %copy-start.6 = (bf16[2,16,256]{2,1,0:T(8,128)(2,1)S(1)}, bf16[2,16,256]{2,1,0:T(8,128)(2,1)}, u32[]{:S(2)}) copy-start(bf16[2,16,256]{2,1,0:T(8,128)(2,1)} %param.29) | copy-start | bytes 49156
  7.2 80.6 %copy-start.16 = (bf16[128]{0:T(256)(128)(2,1)S(1)}, bf16[128]{0:T(256)(128)(2,1)}, u32[]{:S(2)}) copy-start(bf16[128]{0:T(256)(128)(2,1)} %param.22) | copy-start | bytes 772
  7.2 81.2 %copy-start.13 = (s32[1,4,8]{2,1,0:T(4,128)S(1)}, s32[1,4,8]{2,1,0:T(4,128)}, u32[]{:S(2)}) copy-start(s32[1,4,8]{2,1,0:T(4,128)} %param.35) | copy-start | bytes 388
  7.2 85.5 %all-gather.11.cloned.1.call-start = ((), (), s32[]{:S(2)}) async-start(), calls=%async_computation.3 | async-start | bytes 1622016 | tf_op jit(solution)/shard_map/all_gather | solution.py:103
  8.0 148.6 %all-gather.9.cloned.1.call-start = ((), (), s32[]{:S(2)}) async-start(), calls=%async_computation.2 | async-start | bytes 2162688 | tf_op jit(solution)/shard_map/all_gather | solution.py:124
  8.9 215.5 %all-gather.7.cloned.1.call-start = ((), (), s32[]{:S(2)}) async-start(), calls=%async_computation.1 | async-start | bytes 3342336 | tf_op jit(solution)/shard_map/all_gather | solution.py:83
  9.7 299.9 %all-gather.13.cloned.1.call-start = ((), (), s32[]{:S(2)}) async-start(), calls=%async_computation.4 | async-start | bytes 2162688 | tf_op jit(solution)/shard_map/all_gather | solution.py:123
  10.3 359.6 %all-gather.15.cloned.1.call-start = ((), (), s32[]{:S(2)}) async-start(), calls=%async_computation.5 | async-start | bytes 2162688 | tf_op jit(solution)/shard_map/all_gather | solution.py:204
  10.8 450.9 %reduce-scatter.2.cloned.1.call-start = ((), (), s32[]{:S(2)}) async-start(), calls=%async_computation.6 | async-start | bytes 3342336 | tf_op jit(solution)/shard_map/reduce_scatter | solution.py:207
  14.2 147.1 %copy-start.11 = (f32[64]{0:T(128)}, f32[64]{0:T(128)S(1)}, u32[]{:S(2)}) copy-start(f32[64]{0:T(128)S(1)} %multiply_exponential_fusion) | copy-start | bytes 772
  224.4 2.8 copy-start.1
  227.3 2.8 copy-start.5
  227.3 2.8 copy-start.9
  228.4 1.7 copy-start.2
  305.6 3.3 copy-start.14
  305.6 3.4 copy-start.12
  309.6 3.9 copy-start.4
  309.6 4.5 copy-start.15
  314.3 1.2 copy-start.3
  374.1 0.7 copy-start.7
  374.1 30.2 %copy-start.8 = (bf16[2,16,256]{2,1,0:T(8,128)(2,1)S(1)}, bf16[2,16,256]{2,1,0:T(8,128)(2,1)}, u32[]{:S(2)}) copy-start(bf16[2,16,256]{2,1,0:T(8,128)(2,1)} %param.31) | copy-start | bytes 49156
  374.1 60.9 %copy-start.10 = (f32[384,4]{0,1:T(4,128)S(1)}, f32[384,4]{0,1:T(4,128)}, u32[]{:S(2)}) copy-start(f32[384,4]{0,1:T(4,128)} %get-tuple-element.17) | copy-start | bytes 18436
Sparse Core Ops, SparseCore 0:
  10.2 75.3 all-gather.10
  87.7 68.8 all-gather.8
  159.6 64.8 all-gather.6
  226.4 71.1 all-gather.12
  299.5 70.3 all-gather.14
  374.3 87.4 reduce-scatter.1
